TPU v7x, 512 devices: a whole 4x8x8 slice. The times are simulated.
512 devices in a mesh: user: 8 (over z), item: 4 (over x), tm: 16 (over y, core).
Axes of the slice: x: 4, y: 8, z: 8, core: 2. Of those that a mesh axis runs over, the one named last changes fastest.
Arguments:
- blocks: bfloat16 [8, 4, 16, 8, 64, 4096], P('user', 'item', 'tm'), may hold values from 0 to 8
- block_coords: int32 [8, 4, 16, 8, 3], P('user', 'item', 'tm'), may hold values from 0 to 127, as said below
- block_count: int32 [8, 4, 16], P('user', 'item', 'tm'), may hold values from 1 to 8, as said below
- a_factor: float32 [8192, 128], P(('user', 'item', 'tm')), as said below
- item_factor: bfloat16 [4096, 128], P(('item', 'user', 'tm')), as said below
- hour_factor: bfloat16 [8192, 128], P(('tm', 'user', 'item')), as said below
Outputs:
- new_factor: float32 [8192, 128], P(('user', 'item', 'tm'))
Inputs may be any that keep to these rules, and one draw needn't show every extreme that they name: `block_coords`: the user block of a slot of device (u, i, t) lies in u * 16 to u * 16 + 15, its item block in i * 16 to i * 16 + 15, its hour block in t * 8 to t * 8 + 7; the 8 slots of a device name distinct blocks; slots at or past the device's count are not part of the tensor. `block_count`: some device lists all 8 slots. `a_factor`: entries are nonnegative. `item_factor`: entries are positive. `hour_factor`: entries are positive.
All inputs are finite; a program needn't handle non-finite values.
Results may differ from a plain program's by a relative error of at most 0.00045.
Values may be sent and summed in bfloat16 or wider, within the bound.
A program may use at most 64 MiB of HBM per device.

v0:
```python
import jax
import jax.numpy as jnp
from jax import lax
from jax.sharding import PartitionSpec as P


def update_column(factor, mttkrp, gram, column):
    weights = lax.dynamic_index_in_dim(gram, column, 1, keepdims=False)
    pivot = lax.dynamic_index_in_dim(weights, column, 0, keepdims=False)
    current = lax.dynamic_index_in_dim(factor, column, 1, keepdims=False)
    target = lax.dynamic_index_in_dim(mttkrp, column, 1, keepdims=False)
    fitted = jnp.dot(factor, weights, precision=lax.Precision.HIGHEST)
    fresh = jnp.maximum(current + (target - fitted) / pivot, 0.0)
    return lax.dynamic_update_index_in_dim(factor, fresh, column, 1)


def self_product(matrix):
    return lax.dot_general(
        matrix, matrix, (((0,), (0,)), ((), ())), preferred_element_type=jnp.float32
    )


def per_device(blocks, block_coords, block_count, a_factor, item_factor, hour_factor):
    tiles = blocks.reshape(blocks.shape[3:])
    coords = block_coords.reshape(block_coords.shape[3:])
    count = block_count.reshape(())
    width = tiles.shape[1]
    rank = item_factor.shape[1]
    item_slab = lax.all_gather(item_factor, ("user", "tm"), axis=0, tiled=True)
    hour_slab = lax.all_gather(hour_factor, ("user", "item"), axis=0, tiled=True)
    hour_blocks = hour_slab.reshape(hour_slab.shape[0] // width, width, rank)
    share_rows = a_factor.shape[0]
    user_rows = share_rows * lax.axis_size("item") * lax.axis_size("tm")
    user_first = lax.axis_index("user") * (user_rows // width)
    item_first = lax.axis_index("item") * (item_slab.shape[0] // width)
    hour_first = lax.axis_index("tm") * hour_blocks.shape[0]

    def add_block(totals, tile, coord, hour_rows):
        item_rows = lax.dynamic_slice_in_dim(
            item_slab, (coord[1] - item_first) * width, width, 0
        ).astype(jnp.float32)
        khatri = (
            (item_rows[:, None, :] * hour_rows.astype(jnp.float32)[None, :, :])
            .reshape(width * width, rank)
            .astype(jnp.bfloat16)
        )
        term = jnp.dot(tile, khatri, preferred_element_type=jnp.float32)
        start = (coord[0] - user_first) * width
        current = lax.dynamic_slice_in_dim(totals, start, width, 0)
        return lax.dynamic_update_slice_in_dim(totals, current + term, start, 0)

    def own_step(slot, totals):
        tile = lax.dynamic_index_in_dim(tiles, slot, 0, keepdims=False)
        coord = lax.dynamic_index_in_dim(coords, slot, 0, keepdims=False)
        hour_rows = lax.dynamic_index_in_dim(hour_blocks, coord[2] - hour_first, 0, keepdims=False)
        return add_block(totals, tile, coord, hour_rows)

    totals = jnp.zeros((user_rows, rank), jnp.float32)
    totals = lax.fori_loop(0, count, own_step, totals)
    summed = lax.psum(totals, ("item", "tm"))
    position = lax.axis_index("item") * lax.axis_size("tm") + lax.axis_index("tm")
    mttkrp = lax.dynamic_slice_in_dim(summed, position * share_rows, share_rows, 0)
    gram_items, gram_hours = lax.psum(
        (self_product(item_factor), self_product(hour_factor)), ("user", "item", "tm")
    )
    gram = gram_items * gram_hours
    group = 16

    def sweep(block, factor):
        for offset in range(group):
            factor = update_column(factor, mttkrp, gram, block * group + offset)
        return factor

    return lax.fori_loop(0, rank // group, sweep, a_factor)


def solution(mesh):
    placed = (
        P("user", "item", "tm", None, None, None),
        P("user", "item", "tm", None, None),
        P("user", "item", "tm"),
        P(("user", "item", "tm"), None),
        P(("item", "user", "tm"), None),
        P(("tm", "user", "item"), None),
    )
    return jax.shard_map(
        per_device,
        mesh=mesh,
        in_specs=placed,
        out_specs=P(("user", "item", "tm"), None),
        check_vma=False,
    )
```

profile of v0, /device:TPU:2, one launch (start us, length us, event | category | flops | bytes accessed | tf_op | source)
XLA Modules:
  0.0 590.2 jit_solution(8561335520772189482)
XLA Ops:
  6.5 1.6 fusion.118
  8.1 1.6 fusion.119
  9.8 57.2 %all_gather.6 = bf16[1024,128]{1,0:T(8,128)(2,1)S(1)} all-gather(bf16[8,128]{1,0:T(8,128)(2,1)} %param.14), channel_id=1, replica_groups=mesh['user'=8,'item'=4,'tm'=16] {'user','tm'}, dimensions={0}, use_global_device_ids=true | all-gather | bytes 264192 | tf_op jit(solution)/shard_map/all_gather | solution.py:29
  67.0 41.9 %all_gather.7 = bf16[512,128]{1,0:T(8,128)(2,1)S(1)} all-gather(bf16[16,128]{1,0:T(8,128)(2,1)} %param.15), channel_id=1, replica_groups=mesh['user'=8,'item'=4,'tm'=16] {'user','item'}, dimensions={0}, use_global_device_ids=true | all-gather | bytes 135168 | tf_op jit(solution)/shard_map/all_gather | solution.py:30
  109.6 10.6 %while.26 = (s32[]{:T(128)}, f32[1024,128]{1,0:T(8,128)S(1)}, s32[]{:T(128)}, s32[8,3]{0,1:T(4,128)S(1)}, s32[]{:T(128)}, /*index=5*/bf16[8,64,4096]{2,1,0:T(8,1...) while((s32[]{:T(128)}, f32[1024,128]{1,0:T(8,128)S(1)}, ...), condition=%wide.region_3.4_spmd, body=%wide.region_2.3_spmd.sunk | while | flops 68182032 | bytes 2851221 | solution.py:59
  113.2 1.4 fusion.181
  118.1 1.4 fusion.181
  120.1 1.0 copy.7
  121.3 156.1 %all-reduce.6.cloned.1.call-done = (f32[128,128]{1,0:T(8,128)}, f32[128,128]{1,0:T(8,128)}) async-done(((f32[128,128]{1,0:T(8,128)}, f32[128,128]{1,0:T(8,128)}), (f32[128,128]{1,0:T(8,128)}, f32[128,128]{1,0:T(8,128)})) %all-reduce.6.cloned.1.call-update) | async-done | bytes 131088 | tf_op jit(solution)/shard_map/psum | solution.py:63
  277.4 0.9 mul.78
  278.4 190.9 %all-reduce.4.cloned.1.call-done = f32[1024,128]{0,1:T(8,128)} async-done(((f32[1024,128]{0,1:T(8,128)}), f32[1024,128]{0,1:T(8,128)}) %all-reduce.4.cloned.1.call-update) | async-done | bytes 524304 | tf_op jit(solution)/shard_map/psum | solution.py:60
  469.3 0.9 constant_dynamic-slice_fusion.65
  470.2 112.5 %while.27 = (s32[]{:T(128)}, f32[16,128]{0,1:T(8,128)S(1)}, f32[16,128]{0,1:T(8,128)S(1)}, f32[128,128]{0,1:T(8,128)S(1)}, s32[]{:T(128)}, /*index=5*/s32[]{:T(1...) while((s32[]{:T(128)}, f32[16,128]{0,1:T(8,128)S(1)}, ...), condition=%wide.region_6.7_spmd, body=%wide.region_5.6_spmd.sunk | while | flops 394322 | bytes 1094245 | solution.py:74
  473.5 0.9 fusion.202
  474.4 0.9 fusion.203
  476.1 0.8 fusion.205
  479.3 0.8 fusion.209
  481.0 0.8 fusion.211
  482.6 0.8 fusion.213
  487.6 0.9 fusion.202
  488.5 0.9 fusion.203
  490.1 0.8 fusion.205
  491.8 0.8 fusion.207
  493.4 0.8 fusion.209
  495.0 0.8 fusion.211
  496.7 0.8 fusion.213
  501.7 0.9 fusion.202
  502.6 0.9 fusion.203
  504.2 0.8 fusion.205
  505.8 0.8 fusion.207
  507.4 0.8 fusion.209
  509.1 0.8 fusion.211
  510.8 0.8 fusion.213
  515.7 0.9 fusion.202
  516.6 0.9 fusion.203
  518.3 0.8 fusion.205
  519.9 0.8 fusion.207
  521.5 0.8 fusion.209
  523.2 0.8 fusion.211
  524.8 0.8 fusion.213
  529.8 0.9 fusion.202
  530.7 0.9 fusion.203
  532.3 0.8 fusion.205
  535.6 0.8 fusion.209
  537.2 0.8 fusion.211
  538.9 0.8 fusion.213
  543.9 0.9 fusion.202
  544.8 0.9 fusion.203
  546.4 0.8 fusion.205
  549.6 0.8 fusion.209
  551.3 0.8 fusion.211
  553.0 0.8 fusion.213
  557.9 0.9 fusion.202
  558.8 0.9 fusion.203
  560.4 0.8 fusion.205
  563.7 0.8 fusion.209
  565.4 0.8 fusion.211
  567.0 0.8 fusion.213
  572.0 0.9 fusion.202
  572.9 0.9 fusion.203
  574.5 0.8 fusion.205
  577.8 0.8 fusion.209
  579.4 0.8 fusion.211
  581.1 0.8 fusion.213
  (234 shorter events, 72.0 us)
Async XLA Ops:
  6.5 270.9 %all-reduce.6.cloned.1.call-start = ((), (), s32[]{:S(2)}) async-start(), calls=%async_computation.1 | async-start | bytes 262144 | tf_op jit(solution)/shard_map/psum | solution.py:63
  9.7 459.6 %all-reduce.4.cloned.1.call-start = ((), (), s32[]{:S(2)}) async-start(), calls=%async_computation | async-start | bytes 1048576 | tf_op jit(solution)/shard_map/psum | solution.py:60
  109.6 11.6 %copy-start = (f32[16,128]{1,0:T(8,128)S(1)}, f32[16,128]{1,0:T(8,128)}, u32[]{:S(2)}) copy-start(f32[16,128]{1,0:T(8,128)} %param.13) | copy-start | bytes 24580
Sparse Core Ops, SparseCore 0:
  12.6 264.7 all-reduce.5
  281.3 187.9 all-reduce.3
where the time goes:
time: 592 us; the launch traced here: 590 us
  waiting for transfers between devices  347 us (59%)
  matrix products  107 us (18%)
  blocking collectives  99.1 us (17%)
  local copies, waits for them, and re-layouts  14.5 us (2%)
  between operations  13.5 us (2%)
  loops' own time  7.8 us (1%)
    psum x1, waiting for transfers between devices, per_device(): summed = lax.psum(totals, ('item', 'tm'))  191 us
    psum x1, waiting for transfers between devices, per_device(): lax.psum((self_product(item_factor), self_product(hour_factor)), ('user',...  156 us
    dot_general x128, matrix products, update_column(): fitted = jnp.dot(factor, weights, precision=lax.Precision.HIGHEST)  101 us
    all_gather x1, blocking collectives, per_device(): item_slab = lax.all_gather(item_factor, ('user', 'tm'), axis=0, tiled=True)  57.2 us
    all_gather x1, blocking collectives, per_device(): lax.all_gather(hour_factor, ('user', 'item'), axis=0, tiled=True)  41.9 us
  transfers between devices with their start and end apart: 2, of which 2 were waited for; matrix products, arithmetic and copies ran while one was open for 1% of the time, Pallas kernels for 0%

commit v1 on v0

--- a/solution.py
+++ b/solution.py
@@ -60,8 +60,16 @@
     summed = lax.psum(totals, ("item", "tm"))
     position = lax.axis_index("item") * lax.axis_size("tm") + lax.axis_index("tm")
     mttkrp = lax.dynamic_slice_in_dim(summed, position * share_rows, share_rows, 0)
-    gram_items, gram_hours = lax.psum(
-        (self_product(item_factor), self_product(hour_factor)), ("user", "item", "tm")
+
+    def pass_local_data_all(original):
+        axis_tag = "user"
+        bus_axis = ("item", "tm")
+        for num in (axis_tag, bus_axis):
+            original = lax.psum(original, num)
+        return original
+
+    gram_items, gram_hours = pass_local_data_all(
+        (self_product(item_factor), self_product(hour_factor))
     )
     gram = gram_items * gram_hours
     group = 16

time: 592 us -> 463 us (0.78)
  the two profiles are of different devices: /device:TPU:2 before, /device:TPU:1 now
where the time goes in v1:
time: 463 us; the launch traced here: 460 us
  waiting for transfers between devices  227 us (49%)
  matrix products  105 us (23%)
  blocking collectives  94.2 us (20%)
  local copies, waits for them, and re-layouts  13.9 us (3%)
  between operations  13.5 us (3%)
  loops' own time  5.11 us (1%)
    psum x1, waiting for transfers between devices, per_device(): summed = lax.psum(totals, ('item', 'tm'))  227 us
    dot_general x128, matrix products, update_column(): fitted = jnp.dot(factor, weights, precision=lax.Precision.HIGHEST)  101 us
    all_gather x1, blocking collectives, per_device(): item_slab = lax.all_gather(item_factor, ('user', 'tm'), axis=0, tiled=True)  58.6 us
    all_gather x1, blocking collectives, per_device(): lax.all_gather(hour_factor, ('user', 'item'), axis=0, tiled=True)  35.6 us
  transfers between devices with their start and end apart: 2, of which 1 were waited for; matrix products, arithmetic and copies ran while one was open for 1% of the time, Pallas kernels for 0%

profile of v1, /device:TPU:1, one launch (start us, length us, event | category | flops | bytes accessed | tf_op | source)
XLA Modules:
  0.0 460.5 jit_solution(378344251121175964)
XLA Ops:
  6.5 1.6 fusion.118
  8.1 1.6 fusion.119
  9.8 58.6 %all_gather.6 = bf16[1024,128]{1,0:T(8,128)(2,1)S(1)} all-gather(bf16[8,128]{1,0:T(8,128)(2,1)} %param.14), channel_id=1, replica_groups=mesh['user'=8,'item'=4,'tm'=16] {'user','tm'}, dimensions={0}, use_global_device_ids=true | all-gather | bytes 264192 | tf_op jit(solution)/shard_map/all_gather | solution.py:29
  68.3 35.6 %all_gather.7 = bf16[512,128]{1,0:T(8,128)(2,1)S(1)} all-gather(bf16[16,128]{1,0:T(8,128)(2,1)} %param.15), channel_id=1, replica_groups=mesh['user'=8,'item'=4,'tm'=16] {'user','item'}, dimensions={0}, use_global_device_ids=true | all-gather | bytes 135168 | tf_op jit(solution)/shard_map/all_gather | solution.py:30
  104.7 5.5 %while.26 = (s32[]{:T(128)}, f32[1024,128]{1,0:T(8,128)S(1)}, s32[]{:T(128)}, s32[8,3]{0,1:T(4,128)S(1)}, s32[]{:T(128)}, /*index=5*/bf16[8,64,4096]{2,1,0:T(8,1...) while((s32[]{:T(128)}, f32[1024,128]{1,0:T(8,128)S(1)}, ...), condition=%wide.region_5.6_spmd, body=%wide.region_4.5_spmd.sunk | while | flops 68182032 | bytes 2851221 | solution.py:59
  108.2 1.4 fusion.181
  110.2 1.0 copy.7
  111.4 227.2 %all-reduce.5.cloned.1.call-done = (f32[1024,128]{0,1:T(8,128)}, f32[128,128]{1,0:T(8,128)}, f32[128,128]{1,0:T(8,128)}) async-done(((f32[1024,128]{0,1:T(8,128)}, f32[128,128]{1,0:T(8,128)}, f32[128,128]{1,0:T(8,128)}), (f32[1024,128]{0,1:T(8,128)}, f32[128,128]{1,0:T(8,128)}, f32[128,128]{1,0:T(8,128)})) %all-reduce.5.cloned.1.call-update) | async-done | bytes 655376 | tf_op jit(solution)/shard_map/psum | solution.py:60
  338.5 0.9 mul.78
  339.5 0.9 constant_dynamic-slice_fusion.65
  340.4 112.5 %while.27 = (s32[]{:T(128)}, f32[16,128]{0,1:T(8,128)S(1)}, f32[16,128]{0,1:T(8,128)S(1)}, f32[128,128]{0,1:T(8,128)S(1)}, s32[]{:T(128)}, /*index=5*/s32[]{:T(1...) while((s32[]{:T(128)}, f32[16,128]{0,1:T(8,128)S(1)}, ...), condition=%wide.region_8.9_spmd, body=%wide.region_7.8_spmd.sunk | while | flops 394322 | bytes 1094245 | solution.py:82
  343.0 0.8 fusion.201
  345.4 0.9 fusion.204
  346.3 0.9 fusion.205
  347.9 0.8 fusion.207
  349.6 0.8 fusion.209
  351.2 0.8 fusion.211
  352.8 0.8 fusion.213
  357.0 0.8 fusion.201
  359.4 0.9 fusion.204
  360.3 0.9 fusion.205
  362.0 0.8 fusion.207
  363.6 0.8 fusion.209
  365.2 0.8 fusion.211
  366.9 0.8 fusion.213
  371.1 0.8 fusion.201
  373.5 0.9 fusion.204
  374.4 0.9 fusion.205
  376.0 0.8 fusion.207
  377.7 0.8 fusion.209
  379.3 0.8 fusion.211
  380.9 0.8 fusion.213
  387.6 0.9 fusion.204
  388.5 0.9 fusion.205
  390.1 0.8 fusion.207
  391.8 0.8 fusion.209
  393.4 0.8 fusion.211
  395.0 0.8 fusion.213
  399.2 0.8 fusion.201
  401.6 0.9 fusion.204
  402.5 0.9 fusion.205
  404.2 0.8 fusion.207
  405.8 0.8 fusion.209
  407.4 0.8 fusion.211
  409.1 0.8 fusion.213
  413.3 0.8 fusion.201
  415.7 0.9 fusion.204
  416.6 0.9 fusion.205
  418.2 0.8 fusion.207
  419.9 0.8 fusion.209
  421.5 0.8 fusion.211
  423.1 0.8 fusion.213
  429.8 0.9 fusion.204
  430.7 0.9 fusion.205
  432.3 0.8 fusion.207
  434.0 0.8 fusion.209
  435.6 0.8 fusion.211
  437.2 0.8 fusion.213
  443.9 0.9 fusion.204
  444.7 0.9 fusion.205
  446.4 0.8 fusion.207
  448.0 0.8 fusion.209
  449.6 0.8 fusion.211
  451.3 0.8 fusion.213
  (228 shorter events, 69.9 us)
Async XLA Ops:
  6.5 104.7 %all-reduce.7.cloned.1.call-start = ((), (), s32[]{:S(2)}) async-start(), calls=%async_computation.1 | async-start | bytes 262144 | tf_op jit(solution)/shard_map/psum | solution.py:68
  9.7 328.8 %all-reduce.5.cloned.1.call-start = ((), (), s32[]{:S(2)}) async-start(), calls=%async_computation | async-start | bytes 1310720 | tf_op jit(solution)/shard_map/psum | solution.py:60
  104.7 6.6 %copy-start = (f32[16,128]{1,0:T(8,128)S(1)}, f32[16,128]{1,0:T(8,128)}, u32[]{:S(2)}) copy-start(f32[16,128]{1,0:T(8,128)} %param.13) | copy-start | bytes 24580
Sparse Core Ops, SparseCore 0:
  9.8 79.3 all-reduce.6
  111.4 227.1 all-reduce.4
